TPU v7x, 256 devices: a whole 4x4x8 slice. The times are simulated.
256 devices in a mesh: task: 8 (over z_hi, core), row: 8 (over x, z_lo), col: 4 (over y).
Axes of the slice: x: 4, y: 4, z: 8 (z_hi: 4, z_lo: 2; z = z_hi * 2 + z_lo), core: 2. Of those that a mesh axis runs over, the one named last changes fastest.
Arguments:
- activations: bfloat16 [8, 512, 13824], P('task', 'col', 'row'), may hold values from -6 to 6
- weights: bfloat16 [8, 13824, 5120], P('task', 'row', 'col'), may hold values from -0.0625 to 0.0625
- labels: int32 [8, 512], P('task'), may hold values from 0 to 127
- prototypes: bfloat16 [8, 128, 5120], P('task', None, 'col'), may hold values from -6 to 6
Outputs:
- merged: bfloat16 [13824, 5120], P('row', 'col')
- merged_out: bfloat16 [8, 512, 5120], P('task', 'row', 'col')
All inputs are finite; a program needn't handle non-finite values.
Results may differ from a plain program's by a relative error of at most 0.02.
Values may be sent and summed in bfloat16 or wider, within the bound.
A program may use at most 128 MiB of HBM per device.

v0:
```python
import jax
import jax.numpy as jnp
from jax import lax
from jax.sharding import PartitionSpec as P


def class_targets(label_rows, protos):
    count = label_rows.shape[0]
    onehot = (
        label_rows[:, None] == lax.broadcasted_iota(jnp.int32, (count, protos.shape[0]), 1)
    ).astype(jnp.bfloat16)
    return jnp.dot(onehot, protos, preferred_element_type=jnp.float32)


def local(activations, weights, labels, prototypes):
    acts = activations[0]
    weight = weights[0]
    label_row = labels[0]
    protos = prototypes[0]
    full_acts = lax.all_gather(acts, "col", axis=0, tiled=True)
    partial_out = jnp.dot(full_acts, weight, preferred_element_type=jnp.float32)
    output = lax.psum(partial_out.astype(jnp.bfloat16), "row").astype(jnp.float32)
    grad = output - class_targets(label_row, protos)
    gsq = (grad * grad).astype(jnp.bfloat16)
    wide = full_acts.astype(jnp.float32)
    asq = (wide * wide).astype(jnp.bfloat16)
    fisher = lax.dot_general(asq, gsq, (((0,), (0,)), ((), ())), preferred_element_type=jnp.float32)
    weighted = fisher * weight.astype(jnp.float32)
    numer, denom = (
        lax.psum_scatter(weighted, "task", scatter_dimension=0, tiled=True),
        lax.psum_scatter(fisher, "task", scatter_dimension=0, tiled=True),
    )
    piece = (numer / (denom + 1e-06)).astype(jnp.bfloat16)
    merged = lax.all_gather(piece, "task", axis=0, tiled=True)
    result = lax.psum_scatter(
        jnp.dot(full_acts, merged, preferred_element_type=jnp.float32).astype(jnp.bfloat16),
        "row",
        scatter_dimension=0,
        tiled=True,
    )
    return (merged, result[None])


def solution(mesh):
    placed = (
        P("task", "col", "row"),
        P("task", "row", "col"),
        P("task", None),
        P("task", None, "col"),
    )
    return jax.shard_map(
        local,
        mesh=mesh,
        in_specs=placed,
        out_specs=(P("row", "col"), P("task", "row", "col")),
        check_vma=False,
    )
```

profile of v0, /device:TPU:8, one launch (start us, length us, event | category | flops | bytes accessed | tf_op | source)
XLA Modules:
  0.0 475.8 jit_solution(1805810077636972893)
XLA Ops:
  7.2 0.0 all-gather.6.cloned.1.call-start
  7.2 0.7 all-gather.6.cloned.1.call-update
  7.9 0.0 all-reduce.2.cloned.1.call-start
  8.0 38.4 %all-gather.6.cloned.1.call-done = bf16[1,512,1728]{1,2,0:T(8,128)(2,1)} async-done(((bf16[1,128,1728]{1,2,0:T(8,128)(2,1)}), bf16[1,512,1728]{1,2,0:T(8,128)(2,1)}) %all-gather.6.cloned.1.call-update) | async-done | bytes 1769488 | tf_op jit(solution)/shard_map/all_gather | solution.py:20
  46.4 6.6 %fusion.4 = bf16[512,1280]{1,0:T(8,128)(2,1)} fusion(bf16[1,1728,1280]{2,1,0:T(8,128)(2,1)} %param.5, bf16[1,512,1728]{1,2,0:T(8,128)(2,1)} %all-gather.6.cloned.1.call-done), kind=kOutput, calls=%fused_computation.7 | convolution fusion | flops 2265579520 | bytes 7503872 | tf_op jit(solution)/shard_map/dot_general | solution.py:21
  53.0 0.0 all-reduce.2.cloned.1.call-update
  53.0 0.0 reduce-scatter.6.cloned.1.call-start
  53.1 90.5 %all-reduce.2.cloned.1.call-done = bf16[512,1280]{1,0:T(8,128)(2,1)} async-done(((bf16[512,1280]{1,0:T(8,128)(2,1)}), bf16[512,1280]{1,0:T(8,128)(2,1)}) %all-reduce.2.cloned.1.call-update) | async-done | bytes 1310736 | tf_op jit(solution)/shard_map/psum | solution.py:22
  143.6 9.8 %convert_multiply_fusion = (f32[1728,1280]{1,0:T(8,128)}, f32[1728,1280]{1,0:T(8,128)}) fusion(bf16[1,1728,1280]{2,1,0:T(8,128)(2,1)} %param.5, bf16[512,1280]{1,0:T(8,128)(2,1)} %all-reduce.2.cloned.1.call-done, bf16[1,128,1280]{2,1,0:T(8,128)(2,1)S(1)} %copy-done, s32[512]{0:T(512)S(1)} %bitcast.30, bf16[1,512,1728]{1,2,0:T(8,128)(2,1)S(1)} %copy-done.1), kind=kOutput, calls=%fused_computation | convolution fusion | flops 2442461184 | bytes 25528320 | tf_op jit(solution)/shard_map/dot_general | solution.py:27
  153.4 0.0 reduce-scatter.6.cloned.1.call-update
  153.4 0.0 reduce-scatter.8.cloned.1.call-start
  153.4 0.5 reduce-scatter.8.cloned.1.call-update
  154.0 0.0 all-gather.4.cloned.1.call-start
  154.0 96.8 %reduce-scatter.6.cloned.1.call-done = f32[216,1280]{1,0:T(8,128)} async-done(((f32[1728,1280]{1,0:T(8,128)}), f32[216,1280]{1,0:T(8,128)}) %reduce-scatter.6.cloned.1.call-update) | async-done | bytes 1105936 | tf_op jit(solution)/shard_map/reduce_scatter | solution.py:30
  250.8 104.8 %reduce-scatter.8.cloned.1.call-done = f32[216,1280]{1,0:T(8,128)} async-done(((f32[1728,1280]{1,0:T(8,128)}), f32[216,1280]{1,0:T(8,128)}) %reduce-scatter.8.cloned.1.call-update) | async-done | bytes 1105936 | tf_op jit(solution)/shard_map/reduce_scatter | solution.py:31
  355.7 2.5 divide_convert_fusion
  358.2 0.0 reduce-scatter.10.cloned.1.call-start
  358.3 54.9 %all-gather.4.cloned.1.call-done = bf16[1728,1280]{1,0:T(8,128)(2,1)} async-done(((bf16[216,1280]{1,0:T(8,128)(2,1)}), bf16[1728,1280]{1,0:T(8,128)(2,1)}) %all-gather.4.cloned.1.call-update) | async-done | bytes 4423696 | tf_op jit(solution)/shard_map/all_gather | solution.py:34
  413.1 4.8 %fusion.7 = bf16[512,1280]{0,1:T(8,128)(2,1)S(1)} fusion(bf16[1728,1280]{1,0:T(8,128)(2,1)} %all-gather.4.cloned.1.call-done, bf16[1,512,1728]{1,2,0:T(8,128)(2,1)S(1)} %copy-done.1), kind=kOutput, calls=%fused_computation.9 | convolution fusion | flops 2265579520 | bytes 7503872 | tf_op jit(solution)/shard_map/dot_general | solution.py:36
  418.0 1.4 copy.8
  419.4 42.9 %reduce-scatter.10.cloned.1.call-done = bf16[64,1280]{1,0:T(8,128)(2,1)} async-done(((bf16[512,1280]{1,0:T(8,128)(2,1)}), bf16[64,1280]{1,0:T(8,128)(2,1)}) %reduce-scatter.10.cloned.1.call-update) | async-done | bytes 163856
  462.4 1.1 copy.9
  463.5 0.8 copy.7
  464.3 4.6 copy.12
  (8 shorter events, 0.0 us)
Async XLA Ops:
  7.2 136.4 %copy-start = (bf16[1,128,1280]{2,1,0:T(8,128)(2,1)S(1)}, bf16[1,128,1280]{2,1,0:T(8,128)(2,1)}, u32[]{:S(2)}) copy-start(bf16[1,128,1280]{2,1,0:T(8,128)(2,1)} %param.7) | copy-start | bytes 983044
  7.2 39.2 %all-gather.6.cloned.1.call-start = ((), (), s32[]{:S(2)}) async-start(), calls=%async_computation.7 | async-start | bytes 2211840 | tf_op jit(solution)/shard_map/all_gather | solution.py:20
  7.9 135.7 %copy-start.2 = (s32[1,512]{1,0:T(1,128)S(1)}, s32[1,512]{1,0:T(1,128)}, u32[]{:S(2)}) copy-start(s32[1,512]{1,0:T(1,128)} %param.6) | copy-start | bytes 6148
  7.9 135.7 %all-reduce.2.cloned.1.call-start = ((), (), s32[]{:S(2)}) async-start(), calls=%async_computation.3 | async-start | bytes 2621440 | tf_op jit(solution)/shard_map/psum | solution.py:22
  46.4 97.2 %copy-start.1 = (bf16[1,512,1728]{1,2,0:T(8,128)(2,1)S(1)}, bf16[1,512,1728]{1,2,0:T(8,128)(2,1)}, u32[]{:S(2)}) copy-start(bf16[1,512,1728]{1,2,0:T(8,128)(2,1)} %all-gather.6.cloned.1.call-done) | copy-start | bytes 5308420
  53.0 197.8 %reduce-scatter.6.cloned.1.call-start = ((), (), s32[]{:S(2)}) async-start(), calls=%async_computation.4 | async-start | bytes 9953280 | tf_op jit(solution)/shard_map/reduce_scatter | solution.py:30
  153.4 202.3 %reduce-scatter.8.cloned.1.call-start = ((), (), s32[]{:S(2)}) async-start(), calls=%async_computation.5 | async-start | bytes 9953280 | tf_op jit(solution)/shard_map/reduce_scatter | solution.py:31
  154.0 259.2 %all-gather.4.cloned.1.call-start = ((), (), s32[]{:S(2)}) async-start(), calls=%async_computation.6 | async-start | bytes 4976640 | tf_op jit(solution)/shard_map/all_gather | solution.py:34
  358.2 104.1 %reduce-scatter.10.cloned.1.call-start = ((), (), s32[]{:S(2)}) async-start(), calls=%async_computation.8 | async-start | bytes 1474560
Sparse Core Ops, SparseCore 0:
  9.8 36.5 all-gather.5
  53.1 90.4 all-reduce.1
  153.5 97.2 reduce-scatter.5
  253.4 102.1 reduce-scatter.7
  358.3 54.7 all-gather.3
  419.6 42.7 reduce-scatter.9
where the time goes:
time: 476 us
  waiting for transfers between devices  430 us (90%)
  matrix products  21.2 us (4%)
  between operations  14.1 us (3%)
  local copies, waits for them, and re-layouts  8.06 us (2%)
    reduce_scatter x1, waiting for transfers between devices, local(): lax.psum_scatter(fisher, 'task', scatter_dimension=0, tiled=True)  105 us
    reduce_scatter x1, waiting for transfers between devices, local(): lax.psum_scatter(weighted, 'task', scatter_dimension=0, tiled=True)  96.8 us
    psum x1, waiting for transfers between devices, local(): lax.psum(partial_out.astype(jnp.bfloat16), 'row').astype(jnp.float32)  90.5 us
    all_gather x1, waiting for transfers between devices, local(): merged = lax.all_gather(piece, 'task', axis=0, tiled=True)  54.9 us
    unnamed x7, waiting for transfers between devices  44.2 us
    all_gather x1, waiting for transfers between devices, local(): full_acts = lax.all_gather(acts, 'col', axis=0, tiled=True)  38.4 us
    dot_general x1, matrix products, local(): lax.dot_general(asq, gsq, (((0,), (0,)), ((), ())), preferred_element_typ...  9.77 us
  transfers between devices with their start and end apart: 6, of which 6 were waited for; matrix products, arithmetic and copies ran while one was open for 0% of the time, Pallas kernels for 0%

commit v1 on v0

--- a/solution.py
+++ b/solution.py
@@ -17,7 +17,19 @@
     weight = weights[0]
     label_row = labels[0]
     protos = prototypes[0]
-    full_acts = lax.all_gather(acts, "col", axis=0, tiled=True)
+    ways, here, step = (lax.axis_size("col"), lax.axis_index("col"), acts.shape[0])
+    dims = [n * ways if d == 0 else n for d, n in enumerate(acts.shape)]
+    full = lax.dynamic_update_slice_in_dim(jnp.zeros(dims, acts.dtype), acts, here * step, axis=0)
+    going_up = going_down = acts
+    for far in range(1, ways // 2 + 1):
+        going_up = lax.ppermute(going_up, "col", [(d, (d + 1) % ways) for d in range(ways)])
+        full = lax.dynamic_update_slice_in_dim(full, going_up, (here - far) % ways * step, axis=0)
+        if 2 * far < ways:
+            going_down = lax.ppermute(going_down, "col", [(d, (d - 1) % ways) for d in range(ways)])
+            full = lax.dynamic_update_slice_in_dim(
+                full, going_down, (here + far) % ways * step, axis=0
+            )
+    full_acts = full
     partial_out = jnp.dot(full_acts, weight, preferred_element_type=jnp.float32)
     output = lax.psum(partial_out.astype(jnp.bfloat16), "row").astype(jnp.float32)
     grad = output - class_targets(label_row, protos)

time: 476 us -> 458 us (0.962)
  waiting for transfers between devices: 430 us -> 411 us
    unnamed x7 -> x5, waiting for transfers between devices: 44.2 us -> 0.75 us
    reduce_scatter x0 -> x1, waiting for transfers between devices: none -> 42.9 us  [local(): lax.psum_scatter(jnp.dot(full_acts, merged, preferred_element_type=jnp.fl...]
    all_gather x1 -> x0, waiting for transfers between devices: 38.4 us -> none  [local(): full_acts = lax.all_gather(acts, 'col', axis=0, tiled=True)]
    ppermute x0 -> x3, waiting for transfers between devices: none -> 18.6 us  [the longest x2 18.6 us: local(): lax.ppermute(going_up, 'col', [(d, (d + 1) % ways) for d in range(ways)])]
  transfers between devices with their start and end apart: 6 -> 8, of which waited for: 6 -> 7; matrix products, arithmetic and copies ran while one was open for 0% -> 0% of each run, Pallas kernels for 0% -> 0%
where the time goes in v1:
time: 458 us
  waiting for transfers between devices  411 us (90%)
  matrix products  21.6 us (5%)
  between operations  13.9 us (3%)
  local copies, waits for them, and re-layouts  5.2 us (1%)
    reduce_scatter x1, waiting for transfers between devices, local(): lax.psum_scatter(fisher, 'task', scatter_dimension=0, tiled=True)  104 us
    reduce_scatter x1, waiting for transfers between devices, local(): lax.psum_scatter(weighted, 'task', scatter_dimension=0, tiled=True)  96 us
    psum x1, waiting for transfers between devices, local(): lax.psum(partial_out.astype(jnp.bfloat16), 'row').astype(jnp.float32)  91.8 us
    all_gather x1, waiting for transfers between devices, local(): merged = lax.all_gather(piece, 'task', axis=0, tiled=True)  56.4 us
    reduce_scatter x1, waiting for transfers between devices, local(): lax.psum_scatter(jnp.dot(full_acts, merged, preferred_element_type=jnp.fl...  42.9 us
    ppermute x2, waiting for transfers between devices, local(): lax.ppermute(going_up, 'col', [(d, (d + 1) % ways) for d in range(ways)])  18.6 us
    dot_general x1, matrix products, local(): lax.dot_general(asq, gsq, (((0,), (0,)), ((), ())), preferred_element_typ...  9.77 us
  transfers between devices with their start and end apart: 8, of which 7 were waited for; matrix products, arithmetic and copies ran while one was open for 0% of the time, Pallas kernels for 0%

profile of v1, /device:TPU:8, one launch (start us, length us, event | category | flops | bytes accessed | tf_op | source)
XLA Modules:
  0.0 458.2 jit_solution(16461146961834436043)
XLA Ops:
  7.2 1.7 collective-permute-start
  8.9 0.7 collective-permute-start.1
  9.6 0.1 broadcast_in_dim.6
  9.7 0.1 constant_dynamic-update-slice_fusion.3
  9.9 9.5 %collective-permute-done = bf16[128,1728]{0,1:T(8,128)(2,1)S(1)} collective-permute-done((bf16[128,1728]{0,1:T(8,128)(2,1)}, bf16[128,1728]{0,1:T(8,128)(2,1)S(1)}, u32[]{:S(2)}, u32[]{:S(2)}) %collective-permute-start) | collective-permute-done | bytes 442400 | tf_op jit(solution)/shard_map/ppermute | solution.py:25
  19.4 1.6 collective-permute-start.2
  21.0 0.1 constant_dynamic-update-slice_fusion.2
  21.1 0.1 constant_dynamic-update-slice_fusion.1
  21.2 9.0 %collective-permute-done.2 = bf16[128,1728]{0,1:T(8,128)(2,1)S(1)} collective-permute-done((bf16[128,1728]{0,1:T(8,128)(2,1)S(1)}, bf16[128,1728]{0,1:T(8,128)(2,1)S(1)}, u32[]{:S(2)}, u32[]{:S(2)}) %collective-permute-start.2) | collective-permute-done | bytes 442400 | tf_op jit(solution)/shard_map/ppermute | solution.py:25
  30.3 0.1 constant_dynamic-update-slice_fusion
  30.4 5.9 %fusion.2 = bf16[512,1280]{1,0:T(8,128)(2,1)} fusion(bf16[512,1728]{0,1:T(8,128)(2,1)S(1)} %constant_dynamic-update-slice_fusion, bf16[1,1728,1280]{2,1,0:T(8,128)(2,1)} %param.5), kind=kOutput, calls=%fused_computation.4 | convolution fusion | flops 2265579520 | bytes 7503872 | tf_op jit(solution)/shard_map/dot_general | solution.py:33
  36.3 0.0 reduce-scatter.4.cloned.1.call-start
  36.4 91.8 %all-reduce.2.cloned.1.call-done = bf16[512,1280]{1,0:T(8,128)(2,1)} async-done(((bf16[512,1280]{1,0:T(8,128)(2,1)}), bf16[512,1280]{1,0:T(8,128)(2,1)}) %all-reduce.2.cloned.1.call-update) | async-done | bytes 1310736 | tf_op jit(solution)/shard_map/psum | solution.py:34
  128.2 9.8 %convert_multiply_fusion = (f32[1728,1280]{1,0:T(8,128)}, f32[1728,1280]{1,0:T(8,128)}) fusion(bf16[1,1728,1280]{2,1,0:T(8,128)(2,1)} %param.5, bf16[512,1280]{1,0:T(8,128)(2,1)} %all-reduce.2.cloned.1.call-done, bf16[1,128,1280]{2,1,0:T(8,128)(2,1)S(1)} %copy-done, s32[512]{0:T(512)S(1)} %bitcast.21, bf16[512,1728]{0,1:T(8,128)(2,1)S(1)} %constant_dynamic-update-slice_fusion), kind=kOutput, calls=%fused_computation | convolution fusion | flops 2442461184 | bytes 25528320 | tf_op jit(solution)/shard_map/dot_general | solution.py:39
  138.0 0.0 reduce-scatter.6.cloned.1.call-start
  138.0 0.7 reduce-scatter.6.cloned.1.call-update
  138.8 96.0 %reduce-scatter.4.cloned.1.call-done = f32[216,1280]{1,0:T(8,128)} async-done(((f32[1728,1280]{1,0:T(8,128)}), f32[216,1280]{1,0:T(8,128)}) %reduce-scatter.4.cloned.1.call-update) | async-done | bytes 1105936 | tf_op jit(solution)/shard_map/reduce_scatter | solution.py:42
  234.8 104.4 %reduce-scatter.6.cloned.1.call-done = f32[216,1280]{1,0:T(8,128)} async-done(((f32[1728,1280]{1,0:T(8,128)}), f32[216,1280]{1,0:T(8,128)}) %reduce-scatter.6.cloned.1.call-update) | async-done | bytes 1105936 | tf_op jit(solution)/shard_map/reduce_scatter | solution.py:43
  339.2 2.5 divide_convert_fusion
  341.8 0.0 reduce-scatter.8.cloned.1.call-start
  341.8 56.4 %all-gather.2.cloned.1.call-done = bf16[1728,1280]{1,0:T(8,128)(2,1)} async-done(((bf16[216,1280]{1,0:T(8,128)(2,1)}), bf16[1728,1280]{1,0:T(8,128)(2,1)}) %all-gather.2.cloned.1.call-update) | async-done | bytes 4423696 | tf_op jit(solution)/shard_map/all_gather | solution.py:46
  398.2 5.9 %convolution_convert_fusion = bf16[512,1280]{1,0:T(8,128)(2,1)} fusion(bf16[512,1728]{0,1:T(8,128)(2,1)S(1)} %constant_dynamic-update-slice_fusion, bf16[1728,1280]{1,0:T(8,128)(2,1)} %all-gather.2.cloned.1.call-done), kind=kOutput, calls=%fused_computation.5 | convolution fusion | flops 2265579520 | bytes 7503872 | tf_op jit(solution)/shard_map/dot_general | solution.py:48
  404.1 42.9 %reduce-scatter.8.cloned.1.call-done = bf16[64,1280]{1,0:T(8,128)(2,1)} async-done(((bf16[512,1280]{1,0:T(8,128)(2,1)}), bf16[64,1280]{1,0:T(8,128)(2,1)}) %reduce-scatter.8.cloned.1.call-update) | async-done | bytes 163856 | tf_op jit(solution)/shard_map/reduce_scatter | solution.py:47
  447.0 4.6 %copy.12 = bf16[1728,1280]{1,0:T(8,128)(2,1)} copy(bf16[1728,1280]{1,0:T(8,128)(2,1)} %all-gather.2.cloned.1.call-done) | data formatting | bytes 8847360
  (13 shorter events, 0.2 us)
Async XLA Ops:
  7.2 121.0 %copy-start = (bf16[1,128,1280]{2,1,0:T(8,128)(2,1)S(1)}, bf16[1,128,1280]{2,1,0:T(8,128)(2,1)}, u32[]{:S(2)}) copy-start(bf16[1,128,1280]{2,1,0:T(8,128)(2,1)} %param.7) | copy-start | bytes 983044
  7.2 2.5 copy-start.1
  7.2 121.0 %all-reduce.2.cloned.1.call-start = ((), (), s32[]{:S(2)}) async-start(), calls=%async_computation.3 | async-start | bytes 2621440 | tf_op jit(solution)/shard_map/psum | solution.py:34
  7.2 12.2 %collective-permute-start = (bf16[128,1728]{0,1:T(8,128)(2,1)}, bf16[128,1728]{0,1:T(8,128)(2,1)S(1)}, u32[]{:S(2)}, u32[]{:S(2)}) collective-permute-start(bf16[128,1728]{0,1:T(8,128)(2,1)} %bitcast.19), channel_id=1, source_target_pairs={{0,1},{1,2},{2,3},{3,0},{4,5},{5,6},{6,7},{7,4},{8,9},{9,10},{10,1... | collective-permute-start | bytes 1327112 | tf_op jit(solution)/shard_map/ppermute | solution.py:25
  8.9 12.2 %collective-permute-start.1 = (bf16[128,1728]{0,1:T(8,128)(2,1)}, bf16[128,1728]{0,1:T(8,128)(2,1)S(1)}, u32[]{:S(2)}, u32[]{:S(2)}) collective-permute-start(bf16[128,1728]{0,1:T(8,128)(2,1)} %bitcast.20), channel_id=1, source_target_pairs={{0,3},{1,0},{2,1},{3,2},{4,7},{5,4},{6,5},{7,6},{8,11},{9,8},{10,9... | collective-permute-start | bytes 1327112 | tf_op jit(solution)/shard_map/ppermute | solution.py:28
  19.4 10.8 %collective-permute-start.2 = (bf16[128,1728]{0,1:T(8,128)(2,1)S(1)}, bf16[128,1728]{0,1:T(8,128)(2,1)S(1)}, u32[]{:S(2)}, u32[]{:S(2)}) collective-permute-start(bf16[128,1728]{0,1:T(8,128)(2,1)S(1)} %collective-permute-done), channel_id=1, source_target_pairs={{0,1},{1,2},{2,3},{3,0},{4,5},{5,6},{6,7},{7,4},{8,9},{9,10},{10,1... | collective-permute-start | bytes 1327112 | tf_op jit(solution)/shard_map/ppermute | solution.py:25
  30.4 97.8 %copy-start.2 = (s32[1,512]{1,0:T(1,128)S(1)}, s32[1,512]{1,0:T(1,128)}, u32[]{:S(2)}) copy-start(s32[1,512]{1,0:T(1,128)} %param.6) | copy-start | bytes 6148
  36.3 198.4 %reduce-scatter.4.cloned.1.call-start = ((), (), s32[]{:S(2)}) async-start(), calls=%async_computation.4 | async-start | bytes 9953280 | tf_op jit(solution)/shard_map/reduce_scatter | solution.py:42
  138.0 201.2 %reduce-scatter.6.cloned.1.call-start = ((), (), s32[]{:S(2)}) async-start(), calls=%async_computation.5 | async-start | bytes 9953280 | tf_op jit(solution)/shard_map/reduce_scatter | solution.py:43
  138.7 259.4 %all-gather.2.cloned.1.call-start = ((), (), s32[]{:S(2)}) async-start(), calls=%async_computation.6 | async-start | bytes 4976640 | tf_op jit(solution)/shard_map/all_gather | solution.py:46
  341.8 105.3 %reduce-scatter.8.cloned.1.call-start = ((), (), s32[]{:S(2)}) async-start(), calls=%async_computation.7 | async-start | bytes 1474560 | tf_op jit(solution)/shard_map/reduce_scatter | solution.py:47
Sparse Core Ops, SparseCore 0:
  36.5 91.6 all-reduce.1
  138.1 96.6 reduce-scatter.3
  237.5 101.6 reduce-scatter.5
  341.9 56.2 all-gather.1
  404.2 42.7 reduce-scatter.7
